TPU v7x, 32 devices: a whole 2x2x4 slice. The times are simulated.
32 devices in a mesh: clip: 2 (over x), tm: 16 (over z, y, core).
Axes of the slice: x: 2, y: 2, z: 4, core: 2. Of those that a mesh axis runs over, the one named last changes fastest.
Arguments:
- tokens: bfloat16 [32768, 512], P(('clip', 'tm')), parts along dimension 0, may hold values from -6 to 6
- qkv_weight: bfloat16 [512, 1536], replicated, may hold values from -0.25 to 0.25
- out_weight: bfloat16 [512, 1024], replicated, may hold values from -0.25 to 0.25
- conv_weight: bfloat16 [3, 3, 256, 256], replicated, may hold values from -0.125 to 0.125
- norm_gain: float32 [256], replicated, may hold values from 0.25 to 1.75
- norm_bias: float32 [256], replicated, may hold values from -3 to 3
- group_map: int32 [32], P('clip'), parts along dimension 0, may hold values from 0 to 7, as said below
- token_order: int32 [2048], P('clip'), parts along dimension 0, may hold values from 0 to 1023, each once
- valid_frames: int32 [32], P('clip'), parts along dimension 0, may hold values from 1 to 16
Outputs:
- decoded: bfloat16 [32, 32, 128, 256], P('clip', 'tm'), parts along dimension 0
There are 2 independent parts, one for each index of `clip`. A program takes and returns all parts, laid end to end along the dimension named above; an argument that names none is the same for every part. Nothing has to cross between parts.
Inputs may be any that keep to these rules, and one draw needn't show every extreme that they name: `group_map`: never falls from one run to the next, and every group from 0 to 7 holds at least one run.
All inputs are finite; a program needn't handle non-finite values.
Results may differ from a plain program's by a relative error of at most 0.0055.
The roundings to bfloat16 on the way count: a program that leaves them out, or rounds other values in their place, can miss the bound.
Values may be sent and summed in bfloat16 or wider, within the bound.
A program may use at most 64 MiB of HBM per device.

v0:
```python
import jax
import jax.numpy as jnp
from jax import lax
from jax.sharding import PartitionSpec as P

HEADS = 16
NORM_GROUPS = 32


def padded_2(cells, sides, width):
    for axis, dim in sides:
        count = lax.axis_size(axis)
        ends = count - 1
        head = lax.slice_in_dim(cells, 0, width, axis=dim)
        tail = lax.slice_in_dim(cells, cells.shape[dim] - width, cells.shape[dim], axis=dim)
        cells = jnp.concatenate(
            [
                lax.ppermute(tail, axis, [(i, (i + 1) % count) for i in range(ends)]),
                cells,
                lax.ppermute(head, axis, [((i + 1) % count, i) for i in range(ends)]),
            ],
            axis=dim,
        )
    return cells


def group_total(field, group_size):
    return jnp.sum(field, axis=(0, 1, 2)).reshape(NORM_GROUPS, group_size).sum(axis=1)


def local(
    tokens,
    qkv_weight,
    out_weight,
    conv_weight,
    norm_gain,
    norm_bias,
    group_map,
    token_order,
    valid_frames,
):
    tile_count = lax.axis_size("tm")
    device_rank = lax.axis_index("tm")
    token_count, model_width = tokens.shape
    channels = conv_weight.shape[3]
    head_dim = model_width // HEADS
    highest = lax.Precision.HIGHEST
    mixed = jnp.dot(tokens, qkv_weight, preferred_element_type=jnp.float32).astype(jnp.bfloat16)
    query_feats = jax.nn.relu(mixed[:, :model_width]).reshape(token_count, HEADS, head_dim)
    key_feats = jax.nn.relu(mixed[:, model_width : 2 * model_width]).reshape(
        token_count, HEADS, head_dim
    )
    value_rows = mixed[:, 2 * model_width :].reshape(token_count, HEADS, head_dim)
    local_state = jnp.einsum(
        "thk,thv->khv", key_feats, value_rows, preferred_element_type=jnp.float32
    ).reshape(head_dim, model_width)
    local_sum = jnp.sum(key_feats, axis=0, dtype=jnp.float32).reshape(model_width)
    own_group = lax.dynamic_slice_in_dim(group_map, device_rank, 1)
    piece_states = lax.all_gather(local_state[None], "tm", axis=0, tiled=True)
    piece_sums = lax.all_gather(local_sum[None], "tm", axis=0, tiled=True)
    weights = (group_map < own_group).astype(jnp.float32)
    prefix_state = jnp.einsum("c,ckd->kd", weights, piece_states, precision=highest)
    prefix_sum = jnp.dot(weights, piece_sums, precision=highest)
    total_state = (local_state + prefix_state).reshape(head_dim, HEADS, head_dim)
    total_sum = (local_sum + prefix_sum).reshape(HEADS, head_dim)
    query_float = query_feats.astype(jnp.float32)
    numer = jnp.einsum("thk,khv->thv", query_float, total_state, precision=highest)
    denom = jnp.einsum("thk,hk->th", query_float, total_sum, precision=highest) + 1.0
    attended = (numer / denom[:, :, None]).reshape(token_count, model_width).astype(jnp.bfloat16)
    raster = jnp.take(attended, jnp.argsort(token_order), axis=0)
    row_tokens = token_count // tile_count
    mapped = jnp.dot(raster, out_weight, preferred_element_type=jnp.float32).astype(jnp.bfloat16)
    regrouped = mapped.reshape(1, tile_count, row_tokens * 4 * channels)
    tiled = lax.all_to_all(regrouped, "tm", split_axis=1, concat_axis=0, tiled=True)
    shuffled = tiled.reshape(tile_count, 1, row_tokens, 2, 2, channels).transpose(0, 1, 3, 2, 4, 5)
    shuffled = shuffled.reshape(tile_count, 2, 2 * row_tokens, channels)
    own_valid = lax.dynamic_slice_in_dim(valid_frames, device_rank, 1)
    frame_mask = (jnp.arange(tile_count, dtype=jnp.int32) < own_valid)[:, None, None, None]
    shuffled = jnp.where(frame_mask, shuffled, jnp.zeros((), jnp.bfloat16))
    padded = padded_2(shuffled, (("tm", 1),), 1)
    convolved = lax.conv_general_dilated(
        padded,
        conv_weight,
        (1, 1),
        ((0, 0), (1, 1)),
        dimension_numbers=("NHWC", "HWIO", "NHWC"),
        preferred_element_type=jnp.float32,
    )
    convolved = jnp.where(frame_mask, convolved, jnp.zeros((), jnp.float32))
    group_size = channels // NORM_GROUPS
    total_count = jnp.sum(valid_frames).astype(jnp.float32) * (group_size * 4 * row_tokens)
    group_mean = lax.psum(group_total(convolved, group_size), "tm") / total_count
    centred = jnp.where(
        frame_mask, convolved - jnp.repeat(group_mean, group_size), jnp.zeros((), jnp.float32)
    )
    group_var = lax.psum(group_total(centred * centred, group_size), "tm") / total_count
    norm_scale = norm_gain * lax.rsqrt(jnp.repeat(group_var, group_size) + 1e-05)
    normed = centred * norm_scale + norm_bias
    decoded = jnp.where(frame_mask, jax.nn.silu(normed), jnp.zeros((), jnp.float32)).astype(
        jnp.bfloat16
    )
    return decoded


def solution(mesh):
    in_specs = (P(("clip", "tm"), None), P(), P(), P(), P(), P(), P("clip"), P("clip"), P("clip"))
    out_specs = P("clip", "tm", None, None)
    return jax.shard_map(local, mesh=mesh, in_specs=in_specs, out_specs=out_specs, check_vma=False)
```

profile of v0, /device:TPU:0, one launch (start us, length us, event | category | flops | bytes accessed | tf_op | source)
XLA Modules:
  0.0 304.3 jit_solution(946376919256069075)
XLA Ops:
  6.5 0.0 copy-start
  6.5 0.0 all-gather.4.cloned.1.call-start
  6.5 1.4 copy-done
  7.9 3.0 convolution_convert_fusion
  11.0 0.0 copy-start.2
  11.0 1.7 copy-done.2
  12.6 1.7 slice_maximum_fusion
  14.4 1.5 copy.30
  15.9 0.0 copy-start.3
  15.9 2.3 copy.31
  18.2 1.6 fusion.26
  19.8 0.8 copy.32
  20.6 0.0 all-gather.4.cloned.1.call-update
  20.6 0.6 dynamic_slice.7
  21.2 1.5 convert_reduce_fusion
  22.7 23.2 %all-gather.1 = f32[16,1,512]{2,1,0:T(1,128)S(1)} all-gather(f32[1,1,512]{2,1,0:T(1,128)S(1)} %bitcast.63), channel_id=2, replica_groups=mesh['clip'=2,'tm'=16] {'tm'}, dimensions={0}, use_global_device_ids=true | all-gather | bytes 34816 | tf_op jit(solution)/shard_map/all_gather | solution.py:60
  45.9 0.7 fusion.13
  46.6 0.1 reshape.88
  46.6 1.5 copy.33
  48.2 4.4 %sort.17 = (s32[1024]{0:T(1024)}, s32[1024]{0:T(1024)S(1)}) sort(s32[1024]{0:T(1024)S(1)} %copy-done.3, s32[1024]{0:T(1024)S(1)} %iota.10), dimensions={0}, to_apply=%region_0.1 | sort | flops 10240 | bytes 16384 | tf_op jit(solution)/shard_map/jit(argsort)/sort | solution.py:70
  52.5 0.5 fusion.27
  53.1 10.2 %all-gather.4.cloned.1.call-done = f32[16,32,512]{2,1,0:T(8,128)} async-done(((f32[1,32,512]{2,1,0:T(8,128)}), f32[16,32,512]{2,1,0:T(8,128)}) %all-gather.4.cloned.1.call-update) | async-done | bytes 1048592 | tf_op jit(solution)/shard_map/all_gather | solution.py:59
  63.2 2.8 fusion.7
  66.0 0.1 copy.39
  66.2 2.0 fusion.6
  68.2 1.5 copy.34
  69.7 5.1 %gather_fusion = bf16[1024,512]{1,0:T(8,128)(2,1)} fusion(bf16[1024,512]{1,0:T(8,128)(2,1)S(1)} %copy.34, s32[1024]{0:T(1024)S(1)} %fusion.16), kind=kCustom, calls=%fused_computation | custom fusion | bytes 2101248 | tf_op jit(solution)/shard_map/jit(_take)/gather | solution.py:70
  74.8 4.2 %convolution_convert_fusion.1 = bf16[1024,1024]{1,0:T(8,128)(2,1)} fusion(bf16[512,1024]{1,0:T(8,128)(2,1)} %param.11, bf16[1024,512]{1,0:T(8,128)(2,1)} %gather_fusion, pred[1024]{0:T(1024)(128)(4,1)S(1)} %compare_and_fusion), kind=kOutput, calls=%fused_computation.16 | convolution fusion | flops 1075314688 | bytes 4195328 | tf_op jit(solution)/shard_map/dot_general | solution.py:72
  78.9 10.3 %reshape.91 = bf16[1,16,65536]{2,0,1:T(2,128)(2,1)} reshape(bf16[1024,1024]{1,0:T(8,128)(2,1)} %convolution_convert_fusion.1) | data formatting | bytes 4194304 | tf_op jit(solution)/shard_map/reshape | solution.py:73
  89.2 0.5 broadcast.24
  89.7 14.3 %reduce.3 = bf16[16,65536]{1,0:T(8,128)(2,1)} reduce(bf16[16,1,65536]{2,1,0:T(2,128)(2,1)} %bitcast.52, bf16[]{:T(256)} %broadcast.24), dimensions={1}, to_apply=%bitcast.39.reduce_sub_computation | reduce | bytes 4194306
  104.0 4.1 %reshape.93 = bf16[16,2,32768]{2,1,0:T(2,128)(2,1)} reshape(bf16[16,65536]{1,0:T(8,128)(2,1)} %reduce.3) | data formatting | bytes 4194304
  108.1 4.6 %all-to-all-start = ((bf16[16,2,32768]{2,1,0:T(2,128)(2,1)}), bf16[16,2,32768]{2,1,0:T(2,128)(2,1)}, u32[]{:S(2)}, u32[]{:S(2)}) async-start(bf16[16,2,32768]{2,1,0:T(2,128)(2,1)} %reshape.93), calls=%async_computation | async-start | bytes 4194304 | tf_op jit(solution)/shard_map/all_to_all | solution.py:74
  112.7 0.6 dynamic_slice.6
  113.3 0.6 iota_compare_fusion
  114.0 39.5 %all-to-all-done = bf16[16,2,32768]{2,1,0:T(2,128)(2,1)} async-done(((bf16[16,2,32768]{2,1,0:T(2,128)(2,1)}), bf16[16,2,32768]{2,1,0:T(2,128)(2,1)}, u32[]{:S(2)}, u32[]{:S(2)}) %all-to-all-start) | async-done | bytes 2097184 | tf_op jit(solution)/shard_map/all_to_all | solution.py:74
  153.5 10.4 %reshape.94 = bf16[16,1,65536]{2,1,0:T(2,128)(2,1)} reshape(bf16[16,2,32768]{2,1,0:T(2,128)(2,1)} %all-to-all-done) | data formatting | bytes 4194304
  163.9 14.5 %bitcast_reduce_fusion = bf16[16,65536]{1,0:T(8,128)(2,1)} fusion(bf16[16,1,65536]{2,1,0:T(2,128)(2,1)} %reshape.94), kind=kLoop, calls=%fused_computation.45 | loop fusion | bytes 4194304 | tf_op jit(solution)/shard_map/all_to_all | solution.py:74
  178.4 4.0 %reshape.67 = bf16[16,1,64,2,2,256]{5,4,3,2,0,1:T(2,128)(2,1)} reshape(bf16[16,65536]{1,0:T(8,128)(2,1)} %bitcast_reduce_fusion) | data formatting | bytes 4194304 | tf_op jit(solution)/shard_map/reshape | solution.py:75
  182.4 3.8 %copy.36 = bf16[16,1,2,64,2,256]{5,0,4,3,2,1:T(8,128)(2,1)S(1)} copy(bf16[16,1,2,64,2,256]{5,4,2,3,0,1:T(2,128)(2,1)} %bitcast.53) | data formatting | bytes 4194304 | tf_op jit(solution)/shard_map/transpose | solution.py:75
  186.3 0.2 broadcast_select_fusion
  186.5 0.0 copy-start.1
  186.5 1.3 copy-done.1
  187.8 1.1 fusion.25
  188.9 3.9 %collective-permute-start = (bf16[16,1,128,256]{3,0,2,1:T(8,128)(2,1)}, bf16[16,1,128,256]{3,0,2,1:T(8,128)(2,1)}, u32[]{:S(2)}, u32[]{:S(2)}) collective-permute-start(bf16[16,1,128,256]{3,0,2,1:T(8,128)(2,1)} %get-tuple-element.10), channel_id=1, source_target_pairs={{0,1},{1,2},{2,3},{3,4},{4,5},{5,6},{6,7},{7,8},{8,9},{9,10},{10,1... | collective-permute-start | bytes 3145736 | tf_op jit(solution)/shard_map/ppermute | solution.py:18
  192.8 1.3 collective-permute-start.1
  194.1 0.7 reduce_sum.57
  195.5 0.0 collective-permute-done
  195.5 3.0 collective-permute-done.1
  198.5 8.6 %select_reduce_fusion = (f32[256]{0:T(256)S(1)}, f32[16,2,128,256]{3,0,2,1:T(8,128)}) fusion(pred[16]{0:T(512)(128)(4,1)S(1)} %iota_compare_fusion, bf16[3,3,256,256]{3,2,1,0:T(8,128)(2,1)} %param.12, bf16[16,1,128,256]{3,0,2,1:T(8,128)(2,1)} %collective-permute-done.1, bf16[16,2,128,256]{3,0,2,1:T(8,128)(2,1)} %copy-done.1, ...), kind=kOutput, calls=%fused_computation.10 | convolution fusion | flops 4821352448 | bytes 9569296 | tf_op jit(solution)/shard_map/conv_general_dilated | solution.py:81
  207.1 0.1 reshape.69
  207.2 0.1 reduce_sum.56
  207.3 50.9 %psum.14 = f32[32]{0:T(128)S(1)} all-reduce(f32[32]{0:T(128)S(1)} %reduce_sum.56), channel_id=1, replica_groups=mesh['clip'=2,'tm'=16] {'tm'}, use_global_device_ids=true, to_apply=%region_4.5 | all-reduce | flops 32 | bytes 256 | tf_op jit(solution)/shard_map/psum | solution.py:92
  258.3 0.1 broadcast_in_dim.58
  258.3 0.1 sub.10
  258.4 3.1 %multiply_reduce_fusion = f32[256]{0:T(256)S(1)} fusion(f32[16,2,128,256]{3,0,2,1:T(8,128)} %get-tuple-element.13, f32[256]{0:T(256)S(1)} %sub.10, pred[16]{0:T(512)(128)(4,1)S(1)} %iota_compare_fusion), kind=kLoop, calls=%fused_computation.8 | loop fusion | flops 5242624 | bytes 4196368 | tf_op jit(solution)/shard_map/reduce_sum | solution.py:28
  261.5 0.1 reshape.70
  261.6 0.1 reduce_sum.59
  261.7 29.7 %psum.15 = f32[32]{0:T(128)S(1)} all-reduce(f32[32]{0:T(128)S(1)} %reduce_sum.59), channel_id=1, replica_groups=mesh['clip'=2,'tm'=16] {'tm'}, use_global_device_ids=true, to_apply=%region_8.9 | all-reduce | flops 32 | bytes 256 | tf_op jit(solution)/shard_map/psum | solution.py:96
  291.4 0.1 broadcast_in_dim.59
  291.5 0.1 rsqrt.8
  291.6 0.0 copy-done.6
  291.6 3.8 %select_convert_fusion = bf16[16,2,128,256]{3,0,2,1:T(8,128)(2,1)S(1)} fusion(f32[16,2,128,256]{3,0,2,1:T(8,128)} %get-tuple-element.13, f32[256]{0:T(256)S(1)} %copy-done.5, f32[256]{0:T(256)S(1)} %mul.23, f32[256]{0:T(256)S(1)} %sub.10, pred[16]{0:T(512)(128)(4,1)S(1)} %iota_compare_fusion), kind=kLoop, calls=%fused_computation.7 | loop fusion | flops 11534336 | bytes 6294544 | tf_op jit(solution)/shard_map/convert_element_type | solution.py:99
  295.4 2.0 copy.37
  (17 shorter events, 0.1 us)
Async XLA Ops:
  6.5 1.4 copy-start
  6.5 56.7 %all-gather.4.cloned.1.call-start = ((), (), s32[]{:S(2)}) async-start(), calls=%async_computation.1 | async-start | bytes 1114112 | tf_op jit(solution)/shard_map/all_gather | solution.py:59
  11.0 1.7 copy-start.2
  14.4 6.2 %copy-start.4 = (s32[16]{0:T(128)S(1)}, s32[16]{0:T(128)}, u32[]{:S(2)}) copy-start(s32[16]{0:T(128)} %param.15) | copy-start | bytes 196
  15.9 32.3 %copy-start.3 = (s32[1024]{0:T(1024)S(1)}, s32[1024]{0:T(1024)}, u32[]{:S(2)}) copy-start(s32[1024]{0:T(1024)} %param.16) | copy-start | bytes 12292
  104.0 8.7 %copy-start.7 = (s32[16]{0:T(128)S(1)}, s32[16]{0:T(128)}, u32[]{:S(2)}) copy-start(s32[16]{0:T(128)} %param.17) | copy-start | bytes 196
  108.1 45.4 %all-to-all-start = ((bf16[16,2,32768]{2,1,0:T(2,128)(2,1)}), bf16[16,2,32768]{2,1,0:T(2,128)(2,1)}, u32[]{:S(2)}, u32[]{:S(2)}) async-start(bf16[16,2,32768]{2,1,0:T(2,128)(2,1)} %reshape.93), calls=%async_computation | async-start | bytes 4194304 | tf_op jit(solution)/shard_map/all_to_all | solution.py:74
  186.5 1.3 copy-start.1
  188.9 6.6 %collective-permute-start = (bf16[16,1,128,256]{3,0,2,1:T(8,128)(2,1)}, bf16[16,1,128,256]{3,0,2,1:T(8,128)(2,1)}, u32[]{:S(2)}, u32[]{:S(2)}) collective-permute-start(bf16[16,1,128,256]{3,0,2,1:T(8,128)(2,1)} %get-tuple-element.10), channel_id=1, source_target_pairs={{0,1},{1,2},{2,3},{3,4},{4,5},{5,6},{6,7},{7,8},{8,9},{9,10},{10,1... | collective-permute-start | bytes 3145736 | tf_op jit(solution)/shard_map/ppermute | solution.py:18
  192.8 5.7 %collective-permute-start.1 = (bf16[16,1,128,256]{3,0,2,1:T(8,128)(2,1)S(1)}, bf16[16,1,128,256]{3,0,2,1:T(8,128)(2,1)}, u32[]{:S(2)}, u32[]{:S(2)}) collective-permute-start(bf16[16,1,128,256]{3,0,2,1:T(8,128)(2,1)S(1)} %get-tuple-element.11), channel_id=1, source_target_pairs={{1,0},{2,1},{3,2},{4,3},{5,4},{6,5},{7,6},{8,7},{9,8},{10,9},{11,1... | collective-permute-start | bytes 3145736 | tf_op jit(solution)/shard_map/ppermute | solution.py:20
  207.1 84.5 %copy-start.6 = (f32[256]{0:T(256)S(1)}, f32[256]{0:T(256)}, u32[]{:S(2)}) copy-start(f32[256]{0:T(256)} %param.13) | copy-start | bytes 3076
  207.1 84.5 %copy-start.5 = (f32[256]{0:T(256)S(1)}, f32[256]{0:T(256)}, u32[]{:S(2)}) copy-start(f32[256]{0:T(256)} %param.14) | copy-start | bytes 3076
Sparse Core Ops, SparseCore 0:
  20.7 42.5 all-gather.3
where the time goes:
time: 306 us; the launch traced here: 304 us
  blocking collectives  104 us (34%)
  local copies, waits for them, and re-layouts  69.7 us (23%)
  waiting for transfers between devices  52.7 us (17%)
  other arithmetic  30.7 us (10%)
  matrix products  23.4 us (8%)
  between operations  14.3 us (5%)
  starting transfers between devices  9.77 us (3%)
    psum x1, blocking collectives, local(): lax.psum(group_total(convolved, group_size), 'tm') / total_count  50.9 us
    all_to_all x1, waiting for transfers between devices, local(): lax.all_to_all(regrouped, 'tm', split_axis=1, concat_axis=0, tiled=True)  39.5 us
    psum x1, blocking collectives, local(): lax.psum(group_total(centred * centred, group_size), 'tm') / total_count  29.7 us
    all_gather x1, blocking collectives, local(): piece_sums = lax.all_gather(local_sum[None], 'tm', axis=0, tiled=True)  23.2 us
    unnamed x19, local copies, waits for them, and re-layouts  19.4 us
    all_to_all x1, local copies, waits for them, and re-layouts, local(): lax.all_to_all(regrouped, 'tm', split_axis=1, concat_axis=0, tiled=True)  14.5 us
    unnamed x1, other arithmetic  14.3 us
    reshape x1, local copies, waits for them, and re-layouts, local(): regrouped = mapped.reshape(1, tile_count, row_tokens * 4 * channels)  10.3 us
  transfers between devices with their start and end apart: 4, of which 3 were waited for; matrix products, arithmetic and copies ran while one was open for 4% of the time, Pallas kernels for 0%

commit v1 on v0

v1 whole, which is shorter than its diff:
```python
import functools

import jax
import jax.numpy as jnp
from jax import lax
from jax.experimental import pallas as pl
from jax.experimental.pallas import tpu as pltpu
from jax.sharding import PartitionSpec as P

HEADS = 16
NORM_GROUPS = 32
MESH = pl.DeviceIdType.MESH
F32 = jnp.float32
BF16 = jnp.bfloat16
CHUNK = 256
BLOCK = 256


def flat(cells):
    frames, rows, width = cells.shape
    if rows % 16 == 0:
        return cells.reshape(frames * rows, width)
    return cells.astype(F32).reshape(frames * rows, width).astype(BF16)


def mega(
    n,
    tokens_hbm,
    qkv_hbm,
    out_hbm,
    conv_hbm,
    gain_ref,
    bias_ref,
    group_ref,
    order_ref,
    valid_ref,
    decoded_hbm,
    tokens_ref,
    qkv_ref,
    outw_ref,
    convw_ref,
    sent_tokens,
    tile_tokens,
    state_acc,
    sum_acc,
    sent_state,
    all_state,
    running,
    prefix,
    rows_ref,
    cells,
    halo,
    conv_acc,
    stat_acc,
    sent_stat,
    all_stat,
    weave,
    out_buf,
    load_sem,
    tok_send,
    tok_recv,
    st_send,
    st_recv,
    halo_send,
    halo_recv,
    stat_send,
    stat_recv,
    store_sem,
):
    me = lax.axis_index("tm")
    count, width = tokens_ref.shape
    row_tokens = count // n
    chunks = count // CHUNK
    frames_per = CHUNK // row_tokens
    head_dim = width // HEADS
    channels = gain_ref.shape[1]
    blocks = width // BLOCK
    heads_per = BLOCK // head_dim
    group_size = channels // NORM_GROUPS

    loads = [
        pltpu.make_async_copy(a, b, load_sem.at[i])
        for i, (a, b) in enumerate(
            [
                (tokens_hbm, tokens_ref),
                (qkv_hbm, qkv_ref),
                (out_hbm, outw_ref),
                (conv_hbm, convw_ref),
            ]
        )
    ]
    for load in loads:
        load.start()

    barrier = pltpu.get_barrier_semaphore()

    @pl.loop(1, n)
    def _(s):
        pl.semaphore_signal(
            barrier, inc=1, device_id={"tm": lax.rem(me + s, n)}, device_id_type=MESH
        )

    def exchange(s, src, dst, send_sem, recv_sem):
        return pltpu.make_async_remote_copy(
            src_ref=src,
            dst_ref=dst,
            send_sem=send_sem.at[s],
            recv_sem=recv_sem.at[s],
            device_id={"tm": lax.rem(me + s, n)},
            device_id_type=MESH,
        )

    def tok_copy(s):
        return exchange(
            s, sent_tokens.at[lax.rem(me + s, n)], tile_tokens.at[me], tok_send, tok_recv
        )

    def state_copy(s):
        return exchange(s, sent_state, all_state.at[me], st_send, st_recv)

    def stat_copy(s):
        return exchange(s, sent_stat, all_stat.at[me], stat_send, stat_recv)

    loads[0].wait()

    @pl.loop(0, chunks)
    def _(c):
        place = lax.broadcasted_iota(jnp.int32, (CHUNK, count), 0) + c * CHUNK
        pick = jnp.where(order_ref[...] == place, 1.0, 0.0).astype(BF16)
        moved = jnp.dot(pick, tokens_ref[...], preferred_element_type=F32)
        sent_tokens[pl.ds(c * frames_per, frames_per)] = moved.reshape(
            frames_per, row_tokens, width
        ).astype(BF16)

    pl.semaphore_wait(barrier, n - 1)

    @pl.loop(1, n)
    def _(s):
        tok_copy(s).start()

    tile_tokens[me] = sent_tokens[me]

    loads[1].wait()
    state_acc[...] = jnp.zeros_like(state_acc)
    sum_acc[...] = jnp.zeros_like(sum_acc)

    @pl.loop(0, chunks)
    def _(c):
        rows = pl.ds(pl.multiple_of(c * CHUNK, CHUNK), CHUNK)
        mixed = jnp.dot(
            tokens_ref[rows, :], qkv_ref[:, width : 3 * width], preferred_element_type=F32
        ).astype(BF16)
        keys = jnp.maximum(mixed[:, :width], jnp.zeros((), BF16))
        sum_acc[...] += keys.astype(F32).reshape(CHUNK // 8, 8, width).sum(axis=0)
        for b in range(blocks):
            lanes = slice(b * BLOCK, (b + 1) * BLOCK)
            state_acc[b] += lax.dot_general(
                keys[:, lanes],
                mixed[:, width + b * BLOCK : width + (b + 1) * BLOCK],
                (((0,), (0,)), ((), ())),
                preferred_element_type=F32,
            )

    head_row = lax.broadcasted_iota(jnp.int32, (BLOCK, BLOCK), 0) // head_dim
    head_col = lax.broadcasted_iota(jnp.int32, (BLOCK, BLOCK), 1) // head_dim
    same_head = head_row == head_col
    for b in range(blocks):
        own = jnp.where(same_head, state_acc[b], 0.0)
        sent_state[0:head_dim, b * BLOCK : (b + 1) * BLOCK] = (
            own.reshape(heads_per, head_dim, BLOCK).sum(axis=0).astype(BF16)
        )
    key_sum = jnp.sum(sum_acc[...], axis=0, keepdims=True)
    high = key_sum.astype(BF16).astype(F32)
    line = lax.broadcasted_iota(jnp.int32, (16, width), 0)
    sent_state[head_dim : head_dim + 16, :] = jnp.where(
        line == 0, high, jnp.where(line == 1, key_sum - high, 0.0)
    ).astype(BF16)

    @pl.loop(1, n)
    def _(s):
        state_copy(s).start()

    all_state[me] = sent_state[...]

    @pl.loop(1, n)
    def _(s):
        tok_copy(s).wait_recv()

    @pl.loop(0, chunks)
    def _(c):
        rows = pl.ds(pl.multiple_of(c * CHUNK, CHUNK), CHUNK)
        mixed = jnp.dot(
            flat(tile_tokens[pl.ds(c * frames_per, frames_per)]),
            qkv_ref[:, 0:width],
            preferred_element_type=F32,
        ).astype(BF16)
        rows_ref[rows, :] = jnp.maximum(mixed, jnp.zeros((), BF16)).astype(F32)

    @pl.loop(1, n)
    def _(s):
        state_copy(s).wait_recv()

    running[...] = jnp.zeros_like(running)
    prefix[...] = jnp.zeros_like(prefix)
    head_ones = same_head.astype(F32).astype(BF16)

    @pl.loop(0, n)
    def _(f):
        new_group = group_ref[f] != group_ref[jnp.maximum(f - 1, 0)]
        before = jnp.where(new_group, running[...], prefix[...])
        prefix[...] = before
        own = all_state[f].astype(F32)
        running[...] += own
        total = before + own
        state = total[0:head_dim, :]
        key_total = jnp.sum(total[head_dim:, :], axis=0, keepdims=True)
        rows = pl.ds(pl.multiple_of(f * row_tokens, 8), row_tokens)
        query = rows_ref[rows, :]
        scaled = (query * key_total).astype(BF16)
        query = query.astype(BF16)
        for b in range(blocks):
            lanes = slice(b * BLOCK, (b + 1) * BLOCK)
            spread = jnp.concatenate([state[:, lanes]] * heads_per, axis=0)
            spread = jnp.where(same_head, spread, 0.0).astype(BF16)
            numer = jnp.dot(query[:, lanes], spread, preferred_element_type=F32)
            denom = jnp.dot(scaled[:, lanes], head_ones, preferred_element_type=F32) + 1.0
            rows_ref[rows, lanes] = numer / denom

    valid_rows = valid_ref[me] * row_tokens
    loads[2].wait()

    def widen(even, odd):
        column = lax.rem(lax.broadcasted_iota(jnp.int32, even.shape, 0), row_tokens)
        odd_left = jnp.where(column == 0, 0.0, pltpu.roll(odd, 1, 0))
        even_right = jnp.where(column == row_tokens - 1, 0.0, pltpu.roll(even, CHUNK - 1, 0))
        return [x.astype(BF16) for x in (odd_left, even, odd, even_right)]

    def down_copy(c):
        rows = pl.ds(pl.multiple_of(c * CHUNK, CHUNK), CHUNK)
        return pltpu.make_async_remote_copy(
            src_ref=cells.at[1, rows, channels : 3 * channels],
            dst_ref=halo.at[0, rows, :],
            send_sem=halo_send.at[0, c],
            recv_sem=halo_recv.at[0, c],
            device_id={"tm": lax.rem(me + 1, n)},
            device_id_type=MESH,
        )

    def up_copy(c):
        rows = pl.ds(pl.multiple_of(c * CHUNK, CHUNK), CHUNK)
        return pltpu.make_async_remote_copy(
            src_ref=cells.at[0, rows, channels : 3 * channels],
            dst_ref=halo.at[1, rows, :],
            send_sem=halo_send.at[1, c],
            recv_sem=halo_recv.at[1, c],
            device_id={"tm": lax.rem(me + n - 1, n)},
            device_id_type=MESH,
        )

    @pl.loop(0, chunks)
    def _(c):
        rows = pl.ds(pl.multiple_of(c * CHUNK, CHUNK), CHUNK)
        mapped = jnp.dot(
            rows_ref[rows, :].astype(BF16), outw_ref[...], preferred_element_type=F32
        )
        row = lax.broadcasted_iota(jnp.int32, mapped.shape, 0) + c * CHUNK
        mapped = jnp.where(row < valid_rows, mapped, 0.0)
        for a in range(2):
            even = mapped[:, 2 * a * channels : (2 * a + 1) * channels]
            odd = mapped[:, (2 * a + 1) * channels : (2 * a + 2) * channels]
            for i, part in enumerate(widen(even, odd)):
                cells[a, rows, i * channels : (i + 1) * channels] = part

        @pl.when(me < n - 1)
        def _():
            down_copy(c).start()

        @pl.when(me > 0)
        def _():
            up_copy(c).start()

    @pl.when(me == 0)
    def _():
        halo[0] = jnp.zeros(halo.shape[1:], BF16)

    @pl.when(me == n - 1)
    def _():
        halo[1] = jnp.zeros(halo.shape[1:], BF16)

    loads[3].wait()
    reach = 3 * channels

    @pl.loop(0, chunks)
    def _(c):
        rows = pl.ds(pl.multiple_of(c * CHUNK, CHUNK), CHUNK)
        for r in range(2):
            for b in range(2):
                lanes = slice(b * channels, b * channels + reach)
                conv_acc[r, rows, b * channels : (b + 1) * channels] = jnp.dot(
                    cells[0, rows, lanes], convw_ref[1 - r], preferred_element_type=F32
                ) + jnp.dot(cells[1, rows, lanes], convw_ref[2 - r], preferred_element_type=F32)

    stat_acc[...] = jnp.zeros_like(stat_acc)

    @pl.loop(0, chunks)
    def _(c):
        rows = pl.ds(pl.multiple_of(c * CHUNK, CHUNK), CHUNK)

        @pl.when(me > 0)
        def _():
            down_copy(c).wait_recv()

        @pl.when(me < n - 1)
        def _():
            up_copy(c).wait_recv()

        row = lax.broadcasted_iota(jnp.int32, (CHUNK, channels), 0) + c * CHUNK
        for r in range(2):
            edge = halo[r, rows, :].astype(F32)
            parts = widen(edge[:, :channels], edge[:, channels:])
            for b in range(2):
                taps = jnp.concatenate(parts[b : b + 3], axis=1)
                lanes = slice(b * channels, (b + 1) * channels)
                result = conv_acc[r, rows, lanes] + jnp.dot(
                    taps, convw_ref[2 * r], preferred_element_type=F32
                )
                result = jnp.where(row < valid_rows, result, 0.0)
                conv_acc[r, rows, lanes] = result
                stat_acc[0] += result.reshape(CHUNK // 8, 8, channels).sum(axis=0)

    unit = (4 * row_tokens * group_size)
    group_row = lax.broadcasted_iota(jnp.int32, (channels, channels), 0) // group_size
    group_col = lax.broadcasted_iota(jnp.int32, (channels, channels), 1) // group_size
    group_ones = (group_row == group_col).astype(F32)

    def group_total(part):
        sums = jnp.sum(part, axis=0, keepdims=True)
        return jnp.dot(
            jnp.broadcast_to(sums, (8, channels)),
            group_ones,
            precision=lax.Precision.HIGHEST,
            preferred_element_type=F32,
        )

    tile_sum = group_total(stat_acc[0])
    tile_mean = tile_sum[0:1, :] / (valid_ref[me] * unit).astype(F32)

    @pl.loop(0, chunks)
    def _(c):
        rows = pl.ds(pl.multiple_of(c * CHUNK, CHUNK), CHUNK)
        row = lax.broadcasted_iota(jnp.int32, (CHUNK, channels), 0) + c * CHUNK
        for r in range(2):
            for b in range(2):
                lanes = slice(b * channels, (b + 1) * channels)
                off = jnp.where(row < valid_rows, conv_acc[r, rows, lanes] - tile_mean, 0.0)
                stat_acc[1] += (off * off).reshape(CHUNK // 8, 8, channels).sum(axis=0)

    tile_square = group_total(stat_acc[1])
    line = lax.broadcasted_iota(jnp.int32, (8, channels), 0)
    sent_stat[...] = jnp.where(line == 0, tile_sum, tile_square)

    @pl.loop(1, n)
    def _(s):
        stat_copy(s).start()

    all_stat[me] = sent_stat[...]

    @pl.loop(1, n)
    def _(s):
        stat_copy(s).wait_recv()

    def add_sum(t, carry):
        total, units = carry
        return total + all_stat[t, 0:1, :], units + valid_ref[t]

    total, units = lax.fori_loop(
        0, n, add_sum, (jnp.zeros((1, channels), F32), jnp.zeros((), jnp.int32))
    )
    total_count = units.astype(F32) * unit
    mean = total / total_count

    def add_square(t, square):
        size = (valid_ref[t] * unit).astype(F32)
        off = all_stat[t, 0:1, :] / size - mean
        return square + all_stat[t, 1:2, :] + size * (off * off)

    square = lax.fori_loop(0, n, add_square, jnp.zeros((1, channels), F32))
    scale = gain_ref[...] * lax.rsqrt(square / total_count + 1e-05)
    shift = bias_ref[...]

    def store(c):
        frames = pl.ds(c * frames_per, frames_per)
        return pltpu.make_async_copy(out_buf.at[frames], decoded_hbm.at[frames], store_sem.at[c])

    @pl.loop(0, chunks)
    def _(c):
        rows = pl.ds(pl.multiple_of(c * CHUNK, CHUNK), CHUNK)
        frames = pl.ds(c * frames_per, frames_per)
        row = lax.broadcasted_iota(jnp.int32, (CHUNK, channels), 0) + c * CHUNK
        for r in range(2):
            for b in range(2):
                lanes = slice(b * channels, (b + 1) * channels)
                normed = (conv_acc[r, rows, lanes] - mean) * scale + shift
                active = jnp.where(row < valid_rows, normed * jax.nn.sigmoid(normed), 0.0)
                for h in range(0, channels, 128):
                    weave[h // 128, pl.ds(b, CHUNK, 2), :] = active[:, h : h + 128]
            for h in range(0, channels, 128):
                out_buf[frames, r, :, h : h + 128] = (
                    weave[h // 128].reshape(frames_per, 2 * row_tokens, 128).astype(BF16)
                )
        store(c).start()

    @pl.loop(0, chunks)
    def _(c):
        store(c).wait()

        @pl.when(me < n - 1)
        def _():
            down_copy(c).wait_send()

        @pl.when(me > 0)
        def _():
            up_copy(c).wait_send()

    @pl.loop(1, n)
    def _(s):
        tok_copy(s).wait_send()
        state_copy(s).wait_send()
        stat_copy(s).wait_send()


def local(
    tokens,
    qkv_weight,
    out_weight,
    conv_weight,
    norm_gain,
    norm_bias,
    group_map,
    token_order,
    valid_frames,
):
    n = lax.axis_size("tm")
    count, width = tokens.shape
    channels = conv_weight.shape[3]
    row_tokens = count // n
    chunks = count // CHUNK
    state_rows = width // HEADS + 16
    anywhere = pl.BlockSpec(memory_space=pl.ANY)
    vmem = pl.BlockSpec(memory_space=pltpu.VMEM)
    smem = pl.BlockSpec(memory_space=pltpu.SMEM)
    dma = pltpu.SemaphoreType.DMA
    return pl.pallas_call(
        functools.partial(mega, n),
        out_shape=jax.ShapeDtypeStruct((n, 2, 2 * row_tokens, channels), BF16),
        in_specs=[anywhere] * 4 + [vmem, vmem, smem, vmem, smem],
        out_specs=anywhere,
        scratch_shapes=[
            pltpu.VMEM((count, width), BF16),
            pltpu.VMEM((width, 3 * width), BF16),
            pltpu.VMEM((width, 4 * channels), BF16),
            pltpu.VMEM((3, 3 * channels, channels), BF16),
            pltpu.VMEM((n, row_tokens, width), BF16),
            pltpu.VMEM((n, row_tokens, width), BF16),
            pltpu.VMEM((width // BLOCK, BLOCK, BLOCK), F32),
            pltpu.VMEM((8, width), F32),
            pltpu.VMEM((state_rows, width), BF16),
            pltpu.VMEM((n, state_rows, width), BF16),
            pltpu.VMEM((state_rows, width), F32),
            pltpu.VMEM((state_rows, width), F32),
            pltpu.VMEM((count, width), F32),
            pltpu.VMEM((2, count, 4 * channels), BF16),
            pltpu.VMEM((2, count, 2 * channels), BF16),
            pltpu.VMEM((2, count, 2 * channels), F32),
            pltpu.VMEM((2, 8, channels), F32),
            pltpu.VMEM((8, channels), F32),
            pltpu.VMEM((n, 8, channels), F32),
            pltpu.VMEM((channels // 128, 2 * CHUNK, 128), F32),
            pltpu.VMEM((n, 2, 2 * row_tokens, channels), BF16),
            dma((4,)),
            dma((n,)),
            dma((n,)),
            dma((n,)),
            dma((n,)),
            dma((2, chunks)),
            dma((2, chunks)),
            dma((n,)),
            dma((n,)),
            dma((chunks,)),
        ],
        compiler_params=pltpu.CompilerParams(
            collective_id=0, has_side_effects=True, vmem_limit_bytes=60 * 1024 * 1024
        ),
    )(
        tokens,
        qkv_weight,
        out_weight,
        conv_weight.reshape(3, 3 * channels, channels),
        norm_gain[None],
        norm_bias[None],
        group_map,
        token_order[None],
        valid_frames,
    )


def solution(mesh):
    in_specs = (P(("clip", "tm"), None), P(), P(), P(), P(), P(), P("clip"), P("clip"), P("clip"))
    out_specs = P("clip", "tm", None, None)
    return jax.shard_map(local, mesh=mesh, in_specs=in_specs, out_specs=out_specs, check_vma=False)
```

time: 306 us -> 85.7 us (0.28)
  blocking collectives: 104 us -> 0 us
  Pallas kernels: 0 us -> 82.4 us
  local copies, waits for them, and re-layouts: 69.7 us -> 3.13 us
  waiting for transfers between devices: 52.7 us -> 0 us
  other arithmetic: 30.7 us -> 0 us
  matrix products: 23.4 us -> 0 us
  between operations: 14.3 us -> 0.01 us
  starting transfers between devices: 9.77 us -> 0 us
    pallas_call x0 -> x1, Pallas kernels: none -> 82.4 us  [local(): pl.pallas_call(functools.partial(mega, n), out_shape=jax.ShapeDtypeStruct...]
    psum x2 -> x0, blocking collectives: 80.6 us -> none  [the longest x1 50.9 us: local(): lax.psum(group_total(convolved, group_size), 'tm') / total_count]
    all_to_all x1 -> x0, waiting for transfers between devices: 39.5 us -> none  [local(): lax.all_to_all(regrouped, 'tm', split_axis=1, concat_axis=0, tiled=True)]
    all_gather x1 -> x0, blocking collectives: 23.2 us -> none  [local(): piece_sums = lax.all_gather(local_sum[None], 'tm', axis=0, tiled=True)]
    unnamed x19 -> x1, local copies, waits for them, and re-layouts: 19.4 us -> 3.13 us
    dot_general x7 -> x0, matrix products: 14.8 us -> none  [the longest x1 4.17 us: local(): jnp.dot(raster, out_weight, preferred_element_type=jnp.float32)]
    reshape x5 -> x0, local copies, waits for them, and re-layouts: 14.5 us -> none  [the longest x1 10.3 us: local(): regrouped = mapped.reshape(1, tile_count, row_tokens * 4 * channels)]
    all_to_all x1 -> x0, local copies, waits for them, and re-layouts: 14.5 us -> none  [local(): lax.all_to_all(regrouped, 'tm', split_axis=1, concat_axis=0, tiled=True)]
  transfers between devices with their start and end apart: 4 -> 0, of which waited for: 3 -> 0; matrix products, arithmetic and copies ran while one was open for 4% -> 0% of each run, Pallas kernels for 0% -> 0%
where the time goes in v1:
time: 85.7 us; the launch traced here: 85.6 us
  Pallas kernels  82.4 us (96%)
  local copies, waits for them, and re-layouts  3.13 us (4%)
    pallas_call x1, Pallas kernels, local(): pl.pallas_call(functools.partial(mega, n), out_shape=jax.ShapeDtypeStruct...  82.4 us
    unnamed x1, local copies, waits for them, and re-layouts  3.13 us

profile of v1, /device:TPU:0, one launch (start us, length us, event | category | flops | bytes accessed | tf_op | source)
XLA Modules:
  0.0 85.6 jit_solution(17754850908692752432)
XLA Ops:
  0.0 82.4 %shard_map.91 = bf16[16,2,128,256]{3,2,1,0:T(8,128)(2,1)} custom-call(bf16[1024,512]{1,0:T(8,128)(2,1)} %tokens_hbm.1, bf16[512,1536]{1,0:T(8,128)(2,1)} %qkv_hbm.1, bf16[512,1024]{1,0:T(8,128)(2,1)} %out_hbm.1, bf16[3,768,256]{2,1,0:T(8,128)(2,1)} %bitcast.4, f32[1,256]{1,0:T(1,128)} %bitcast.6, f32[1,256]{1,0:T(1,128)} %bitcast.7, s32[16]{0:T(128)} %group_ref.1, ...), custom_call_target="tpu_custom_call" | custom-call | tf_op jit(solution)/shard_map/pallas_call | solution.py:453
  82.4 3.1 %copy.11 = bf16[16,2,128,256]{3,2,1,0:T(8,128)(2,1)} copy(bf16[16,2,128,256]{3,2,1,0:T(8,128)(2,1)} %shard_map.91) | data formatting | bytes 4194304

commit v2 on v1

--- a/solution.py
+++ b/solution.py
@@ -30,11 +30,11 @@
     out_hbm,
     conv_hbm,
     gain_ref,
-    bias_ref,
     group_ref,
     order_ref,
     valid_ref,
-    decoded_hbm,
+    conv_out,
+    norm_ref,
     tokens_ref,
     qkv_ref,
     outw_ref,
@@ -45,6 +45,7 @@
     sum_acc,
     sent_state,
     all_state,
+    all_total,
     running,
     prefix,
     rows_ref,
@@ -54,13 +55,14 @@
     stat_acc,
     sent_stat,
     all_stat,
-    weave,
     out_buf,
     load_sem,
     tok_send,
     tok_recv,
     st_send,
     st_recv,
+    pass_send,
+    pass_recv,
     halo_send,
     halo_recv,
     stat_send,
@@ -110,36 +112,66 @@
             device_id_type=MESH,
         )
 
-    def tok_copy(s):
-        return exchange(
-            s, sent_tokens.at[lax.rem(me + s, n)], tile_tokens.at[me], tok_send, tok_recv
-        )
-
-    def state_copy(s):
-        return exchange(s, sent_state, all_state.at[me], st_send, st_recv)
+    def tok_copy(t):
+        return pltpu.make_async_remote_copy(
+            src_ref=sent_tokens.at[t],
+            dst_ref=tile_tokens.at[me],
+            send_sem=tok_send.at[t],
+            recv_sem=tok_recv.at[me],
+            device_id={"tm": t},
+            device_id_type=MESH,
+        )
+
+    def tok_arrival(t):
+        return pltpu.make_async_remote_copy(
+            src_ref=sent_tokens.at[t],
+            dst_ref=tile_tokens.at[t],
+            send_sem=tok_send.at[t],
+            recv_sem=tok_recv.at[t],
+            device_id={"tm": t},
+            device_id_type=MESH,
+        )
+
+    partner = me + 1 - 2 * lax.rem(me, 2)
+
+    def state_copy(k):
+        return pltpu.make_async_remote_copy(
+            src_ref=sent_state,
+            dst_ref=all_state.at[me],
+            send_sem=st_send.at[k],
+            recv_sem=st_recv.at[k],
+            device_id={"tm": lax.rem(me + 2 * k, n)},
+            device_id_type=MESH,
+        )
+
+    def state_pass(k):
+        source = lax.rem(me + n - 2 * k, n)
+        return pltpu.make_async_remote_copy(
+            src_ref=all_state.at[source],
+            dst_ref=all_state.at[source],
+            send_sem=pass_send.at[k],
+            recv_sem=pass_recv.at[k],
+            device_id={"tm": partner},
+            device_id_type=MESH,
+        )
+
+    own_pass = pltpu.make_async_remote_copy(
+        src_ref=sent_state,
+        dst_ref=all_state.at[me],
+        send_sem=pass_send.at[0],
+        recv_sem=pass_recv.at[0],
+        device_id={"tm": partner},
+        device_id_type=MESH,
+    )
 
     def stat_copy(s):
         return exchange(s, sent_stat, all_stat.at[me], stat_send, stat_recv)
 
+    half = chunks // 2
+    near = lax.div(me, n // 2) * half
+    far = half - near
+
     loads[0].wait()
-
-    @pl.loop(0, chunks)
-    def _(c):
-        place = lax.broadcasted_iota(jnp.int32, (CHUNK, count), 0) + c * CHUNK
-        pick = jnp.where(order_ref[...] == place, 1.0, 0.0).astype(BF16)
-        moved = jnp.dot(pick, tokens_ref[...], preferred_element_type=F32)
-        sent_tokens[pl.ds(c * frames_per, frames_per)] = moved.reshape(
-            frames_per, row_tokens, width
-        ).astype(BF16)
-
-    pl.semaphore_wait(barrier, n - 1)
-
-    @pl.loop(1, n)
-    def _(s):
-        tok_copy(s).start()
-
-    tile_tokens[me] = sent_tokens[me]
-
     loads[1].wait()
     state_acc[...] = jnp.zeros_like(state_acc)
     sum_acc[...] = jnp.zeros_like(sum_acc)
@@ -164,45 +196,65 @@
     head_row = lax.broadcasted_iota(jnp.int32, (BLOCK, BLOCK), 0) // head_dim
     head_col = lax.broadcasted_iota(jnp.int32, (BLOCK, BLOCK), 1) // head_dim
     same_head = head_row == head_col
+    pieces = width // 128
     for b in range(blocks):
         own = jnp.where(same_head, state_acc[b], 0.0)
-        sent_state[0:head_dim, b * BLOCK : (b + 1) * BLOCK] = (
-            own.reshape(heads_per, head_dim, BLOCK).sum(axis=0).astype(BF16)
-        )
+        own = own.reshape(heads_per, head_dim, BLOCK).sum(axis=0).astype(BF16)
+        for i in range(BLOCK // 128):
+            at = (b * (BLOCK // 128) + i) * head_dim
+            sent_state[at : at + head_dim, :] = own[:, i * 128 : (i + 1) * 128]
     key_sum = jnp.sum(sum_acc[...], axis=0, keepdims=True)
     high = key_sum.astype(BF16).astype(F32)
-    line = lax.broadcasted_iota(jnp.int32, (16, width), 0)
-    sent_state[head_dim : head_dim + 16, :] = jnp.where(
-        line == 0, high, jnp.where(line == 1, key_sum - high, 0.0)
-    ).astype(BF16)
-
-    @pl.loop(1, n)
-    def _(s):
-        state_copy(s).start()
-
+    line = lax.broadcasted_iota(jnp.int32, (16, 128), 0)
+    packed = jnp.zeros((16, 128), F32)
+    for i in range(pieces):
+        lanes = slice(i * 128, (i + 1) * 128)
+        packed = jnp.where(line == i, high[:, lanes], packed)
+        packed = jnp.where(line == pieces + i, (key_sum - high)[:, lanes], packed)
+    sum_at = pieces * head_dim
+    sent_state[sum_at : sum_at + 16, :] = packed.astype(BF16)
+
+    pl.semaphore_wait(barrier, n - 1)
+
+    @pl.loop(1, n // 2)
+    def _(k):
+        state_copy(k).start()
+
+    own_pass.start()
     all_state[me] = sent_state[...]
 
-    @pl.loop(1, n)
-    def _(s):
-        tok_copy(s).wait_recv()
-
     @pl.loop(0, chunks)
-    def _(c):
-        rows = pl.ds(pl.multiple_of(c * CHUNK, CHUNK), CHUNK)
-        mixed = jnp.dot(
-            flat(tile_tokens[pl.ds(c * frames_per, frames_per)]),
-            qkv_ref[:, 0:width],
-            preferred_element_type=F32,
+    def _(to):
+        place = lax.broadcasted_iota(jnp.int32, (CHUNK, count), 0) + to * CHUNK
+        pick = jnp.where(order_ref[...] == place, 1.0, 0.0).astype(BF16)
+        moved = jnp.dot(pick, tokens_ref[...], preferred_element_type=F32)
+        sent_tokens[pl.ds(to * frames_per, frames_per)] = moved.reshape(
+            frames_per, row_tokens, width
         ).astype(BF16)
-        rows_ref[rows, :] = jnp.maximum(mixed, jnp.zeros((), BF16)).astype(F32)
-
-    @pl.loop(1, n)
-    def _(s):
-        state_copy(s).wait_recv()
+
+    for first in (far, near):
+
+        @pl.loop(0, n // 2)
+        def _(k):
+            t = first * frames_per + lax.rem(me + k, n // 2)
+
+            @pl.when(t != me)
+            def _():
+                tok_copy(t).start()
+
+    tile_tokens[me] = sent_tokens[me]
+
+    @pl.loop(1, n // 2)
+    def _(k):
+        state_copy(k).wait_recv()
+        state_pass(k).start()
+
+    @pl.loop(0, n // 2)
+    def _(k):
+        state_pass(k).wait_recv()
 
     running[...] = jnp.zeros_like(running)
     prefix[...] = jnp.zeros_like(prefix)
-    head_ones = same_head.astype(F32).astype(BF16)
 
     @pl.loop(0, n)
     def _(f):
@@ -211,20 +263,7 @@
         prefix[...] = before
         own = all_state[f].astype(F32)
         running[...] += own
-        total = before + own
-        state = total[0:head_dim, :]
-        key_total = jnp.sum(total[head_dim:, :], axis=0, keepdims=True)
-        rows = pl.ds(pl.multiple_of(f * row_tokens, 8), row_tokens)
-        query = rows_ref[rows, :]
-        scaled = (query * key_total).astype(BF16)
-        query = query.astype(BF16)
-        for b in range(blocks):
-            lanes = slice(b * BLOCK, (b + 1) * BLOCK)
-            spread = jnp.concatenate([state[:, lanes]] * heads_per, axis=0)
-            spread = jnp.where(same_head, spread, 0.0).astype(BF16)
-            numer = jnp.dot(query[:, lanes], spread, preferred_element_type=F32)
-            denom = jnp.dot(scaled[:, lanes], head_ones, preferred_element_type=F32) + 1.0
-            rows_ref[rows, lanes] = numer / denom
+        all_total[f] = before + own
 
     valid_rows = valid_ref[me] * row_tokens
     loads[2].wait()
@@ -257,12 +296,65 @@
             device_id_type=MESH,
         )
 
-    @pl.loop(0, chunks)
-    def _(c):
+    head_ones = same_head.astype(F32).astype(BF16)
+    reach = 3 * channels
+    loads[3].wait()
+
+    def advance(c):
         rows = pl.ds(pl.multiple_of(c * CHUNK, CHUNK), CHUNK)
-        mapped = jnp.dot(
-            rows_ref[rows, :].astype(BF16), outw_ref[...], preferred_element_type=F32
-        )
+
+        @pl.loop(0, frames_per)
+        def _(k):
+            t = c * frames_per + k
+
+            @pl.when(t != me)
+            def _():
+                tok_arrival(t).wait_recv()
+
+        mixed = jnp.dot(
+            flat(tile_tokens[pl.ds(c * frames_per, frames_per)]),
+            qkv_ref[:, 0:width],
+            preferred_element_type=F32,
+        ).astype(BF16)
+        rows_ref[...] = jnp.maximum(mixed, jnp.zeros((), BF16)).astype(F32)
+
+        def attend(k, carry):
+            f = c * frames_per + k
+            total = all_total[f]
+            key_total = jnp.concatenate(
+                [
+                    total[sum_at + i : sum_at + i + 1, :]
+                    + total[sum_at + pieces + i : sum_at + pieces + i + 1, :]
+                    for i in range(pieces)
+                ],
+                axis=1,
+            )
+            here = pl.ds(pl.multiple_of(k * row_tokens, 8), row_tokens)
+            query = rows_ref[here, :]
+            scaled = (query * key_total).astype(BF16)
+            query = query.astype(BF16)
+            for b in range(blocks):
+                lanes = slice(b * BLOCK, (b + 1) * BLOCK)
+                first = b * (BLOCK // 128)
+                state = jnp.concatenate(
+                    [
+                        total[i * head_dim : (i + 1) * head_dim, :]
+                        for i in range(first, first + BLOCK // 128)
+                    ],
+                    axis=1,
+                )
+                high = state.astype(BF16).astype(F32)
+                numer = jnp.zeros((row_tokens, BLOCK), F32)
+                for part in (high, state - high):
+                    spread = jnp.concatenate([part] * heads_per, axis=0)
+                    spread = jnp.where(same_head, spread, 0.0).astype(BF16)
+                    numer += jnp.dot(query[:, lanes], spread, preferred_element_type=F32)
+                denom = jnp.dot(scaled[:, lanes], head_ones, preferred_element_type=F32) + 1.0
+                rows_ref[here, lanes] = numer / denom
+            return carry
+
+        lax.fori_loop(0, frames_per, attend, 0, unroll=frames_per <= 4)
+        mapped = jnp.dot(rows_ref[...].astype(BF16), outw_ref[...], preferred_element_type=F32)
         row = lax.broadcasted_iota(jnp.int32, mapped.shape, 0) + c * CHUNK
         mapped = jnp.where(row < valid_rows, mapped, 0.0)
         for a in range(2):
@@ -279,26 +371,38 @@
         def _():
             up_copy(c).start()
 
-    @pl.when(me == 0)
-    def _():
-        halo[0] = jnp.zeros(halo.shape[1:], BF16)
-
-    @pl.when(me == n - 1)
-    def _():
-        halo[1] = jnp.zeros(halo.shape[1:], BF16)
-
-    loads[3].wait()
-    reach = 3 * channels
-
-    @pl.loop(0, chunks)
-    def _(c):
-        rows = pl.ds(pl.multiple_of(c * CHUNK, CHUNK), CHUNK)
         for r in range(2):
             for b in range(2):
                 lanes = slice(b * channels, b * channels + reach)
                 conv_acc[r, rows, b * channels : (b + 1) * channels] = jnp.dot(
                     cells[0, rows, lanes], convw_ref[1 - r], preferred_element_type=F32
                 ) + jnp.dot(cells[1, rows, lanes], convw_ref[2 - r], preferred_element_type=F32)
+
+    @pl.loop(0, half)
+    def _(k):
+        advance(near + k)
+
+    @pl.loop(0, half)
+    def _(k):
+        advance(far + k)
+
+    @pl.when(me == 0)
+    def _():
+        halo[0] = jnp.zeros(halo.shape[1:], BF16)
+
+    @pl.when(me == n - 1)
+    def _():
+        halo[1] = jnp.zeros(halo.shape[1:], BF16)
+
+    def store(f, r, h):
+        pixels = pl.ds(pl.multiple_of(f * 2 * row_tokens, 8), 2 * row_tokens)
+        return pltpu.make_async_copy(
+            out_buf.at[r, h, pixels, :],
+            conv_out.at[f, r, :, h * 128 : (h + 1) * 128],
+            store_sem.at[f, r, h],
+        )
+
+    sides = [(r, h) for r in range(2) for h in range(channels // 128)]
 
     stat_acc[...] = jnp.zeros_like(stat_acc)
 
@@ -325,8 +429,16 @@
                     taps, convw_ref[2 * r], preferred_element_type=F32
                 )
                 result = jnp.where(row < valid_rows, result, 0.0)
-                conv_acc[r, rows, lanes] = result
+                for h in range(0, channels, 128):
+                    out_buf[r, h // 128, pl.ds(c * 2 * CHUNK + b, CHUNK, 2), :] = result[
+                        :, h : h + 128
+                    ]
                 stat_acc[0] += result.reshape(CHUNK // 8, 8, channels).sum(axis=0)
+
+    @pl.loop(0, n)
+    def _(f):
+        for r, h in sides:
+            store(f, r, h).start()
 
     unit = (4 * row_tokens * group_size)
     group_row = lax.broadcasted_iota(jnp.int32, (channels, channels), 0) // group_size
@@ -345,15 +457,14 @@
     tile_sum = group_total(stat_acc[0])
     tile_mean = tile_sum[0:1, :] / (valid_ref[me] * unit).astype(F32)
 
-    @pl.loop(0, chunks)
+    @pl.loop(0, 2 * chunks)
     def _(c):
-        rows = pl.ds(pl.multiple_of(c * CHUNK, CHUNK), CHUNK)
-        row = lax.broadcasted_iota(jnp.int32, (CHUNK, channels), 0) + c * CHUNK
-        for r in range(2):
-            for b in range(2):
-                lanes = slice(b * channels, (b + 1) * channels)
-                off = jnp.where(row < valid_rows, conv_acc[r, rows, lanes] - tile_mean, 0.0)
-                stat_acc[1] += (off * off).reshape(CHUNK // 8, 8, channels).sum(axis=0)
+        pixels = pl.ds(pl.multiple_of(c * CHUNK, CHUNK), CHUNK)
+        row = lax.broadcasted_iota(jnp.int32, (CHUNK, 128), 0) + c * CHUNK
+        for r, h in sides:
+            lanes = slice(h * 128, (h + 1) * 128)
+            off = jnp.where(row < 2 * valid_rows, out_buf[r, h, pixels, :] - tile_mean[:, lanes], 0.0)
+            stat_acc[1, :, lanes] += (off * off).reshape(CHUNK // 8, 8, 128).sum(axis=0)
 
     tile_square = group_total(stat_acc[1])
     line = lax.broadcasted_iota(jnp.int32, (8, channels), 0)
@@ -386,34 +497,17 @@
 
     square = lax.fori_loop(0, n, add_square, jnp.zeros((1, channels), F32))
     scale = gain_ref[...] * lax.rsqrt(square / total_count + 1e-05)
-    shift = bias_ref[...]
-
-    def store(c):
-        frames = pl.ds(c * frames_per, frames_per)
-        return pltpu.make_async_copy(out_buf.at[frames], decoded_hbm.at[frames], store_sem.at[c])
+    norm_ref[...] = jnp.where(
+        line == 0, mean, jnp.where(line == 1, scale, valid_ref[me].astype(F32))
+    )
+
+    @pl.loop(0, n)
+    def _(f):
+        for r, h in sides:
+            store(f, r, h).wait()
 
     @pl.loop(0, chunks)
     def _(c):
-        rows = pl.ds(pl.multiple_of(c * CHUNK, CHUNK), CHUNK)
-        frames = pl.ds(c * frames_per, frames_per)
-        row = lax.broadcasted_iota(jnp.int32, (CHUNK, channels), 0) + c * CHUNK
-        for r in range(2):
-            for b in range(2):
-                lanes = slice(b * channels, (b + 1) * channels)
-                normed = (conv_acc[r, rows, lanes] - mean) * scale + shift
-                active = jnp.where(row < valid_rows, normed * jax.nn.sigmoid(normed), 0.0)
-                for h in range(0, channels, 128):
-                    weave[h // 128, pl.ds(b, CHUNK, 2), :] = active[:, h : h + 128]
-            for h in range(0, channels, 128):
-                out_buf[frames, r, :, h : h + 128] = (
-                    weave[h // 128].reshape(frames_per, 2 * row_tokens, 128).astype(BF16)
-                )
-        store(c).start()
-
-    @pl.loop(0, chunks)
-    def _(c):
-        store(c).wait()
-
         @pl.when(me < n - 1)
         def _():
             down_copy(c).wait_send()
@@ -424,9 +518,15 @@
 
     @pl.loop(1, n)
     def _(s):
-        tok_copy(s).wait_send()
-        state_copy(s).wait_send()
+        tok_copy(lax.rem(me + s, n)).wait_send()
         stat_copy(s).wait_send()
+
+    own_pass.wait_send()
+
+    @pl.loop(1, n // 2)
+    def _(k):
+        state_copy(k).wait_send()
+        state_pass(k).wait_send()
 
 
 def local(
@@ -445,16 +545,19 @@
     channels = conv_weight.shape[3]
     row_tokens = count // n
     chunks = count // CHUNK
-    state_rows = width // HEADS + 16
+    state_shape = (width // 128 * (width // HEADS) + 16, 128)
     anywhere = pl.BlockSpec(memory_space=pl.ANY)
     vmem = pl.BlockSpec(memory_space=pltpu.VMEM)
     smem = pl.BlockSpec(memory_space=pltpu.SMEM)
     dma = pltpu.SemaphoreType.DMA
-    return pl.pallas_call(
+    conv, norm = pl.pallas_call(
         functools.partial(mega, n),
-        out_shape=jax.ShapeDtypeStruct((n, 2, 2 * row_tokens, channels), BF16),
-        in_specs=[anywhere] * 4 + [vmem, vmem, smem, vmem, smem],
-        out_specs=anywhere,
+        out_shape=(
+            jax.ShapeDtypeStruct((n, 2, 2 * row_tokens, channels), F32),
+            jax.ShapeDtypeStruct((8, channels), F32),
+        ),
+        in_specs=[anywhere] * 4 + [vmem, smem, vmem, smem],
+        out_specs=(anywhere, vmem),
         scratch_shapes=[
             pltpu.VMEM((count, width), BF16),
             pltpu.VMEM((width, 3 * width), BF16),
@@ -464,29 +567,31 @@
             pltpu.VMEM((n, row_tokens, width), BF16),
             pltpu.VMEM((width // BLOCK, BLOCK, BLOCK), F32),
             pltpu.VMEM((8, width), F32),
-            pltpu.VMEM((state_rows, width), BF16),
-            pltpu.VMEM((n, state_rows, width), BF16),
-            pltpu.VMEM((state_rows, width), F32),
-            pltpu.VMEM((state_rows, width), F32),
-            pltpu.VMEM((count, width), F32),
+            pltpu.VMEM(state_shape, BF16),
+            pltpu.VMEM((n,) + state_shape, BF16),
+            pltpu.VMEM((n,) + state_shape, F32),
+            pltpu.VMEM(state_shape, F32),
+            pltpu.VMEM(state_shape, F32),
+            pltpu.VMEM((CHUNK, width), F32),
             pltpu.VMEM((2, count, 4 * channels), BF16),
             pltpu.VMEM((2, count, 2 * channels), BF16),
             pltpu.VMEM((2, count, 2 * channels), F32),
             pltpu.VMEM((2, 8, channels), F32),
             pltpu.VMEM((8, channels), F32),
             pltpu.VMEM((n, 8, channels), F32),
-            pltpu.VMEM((channels // 128, 2 * CHUNK, 128), F32),
-            pltpu.VMEM((n, 2, 2 * row_tokens, channels), BF16),
+            pltpu.VMEM((2, channels // 128, 2 * count, 128), F32),
             dma((4,)),
             dma((n,)),
             dma((n,)),
-            dma((n,)),
-            dma((n,)),
+            dma((n // 2,)),
+            dma((n // 2,)),
+            dma((n // 2,)),
+            dma((n // 2,)),
             dma((2, chunks)),
             dma((2, chunks)),
             dma((n,)),
             dma((n,)),
-            dma((chunks,)),
+            dma((n, 2, channels // 128)),
         ],
         compiler_params=pltpu.CompilerParams(
             collective_id=0, has_side_effects=True, vmem_limit_bytes=60 * 1024 * 1024
@@ -497,11 +602,13 @@
         out_weight,
         conv_weight.reshape(3, 3 * channels, channels),
         norm_gain[None],
-        norm_bias[None],
         group_map,
         token_order[None],
         valid_frames,
     )
+    frame = lax.broadcasted_iota(jnp.int32, conv.shape, 0).astype(F32)
+    normed = (conv - norm[0]) * norm[1] + norm_bias
+    return jnp.where(frame < norm[2], jax.nn.silu(normed), 0.0).astype(BF16)
 
 
 def solution(mesh):

time: 85.7 us -> 74.2 us (0.87)
  Pallas kernels: 82.4 us -> 68.3 us
  other arithmetic: 0 us -> 4.9 us
  local copies, waits for them, and re-layouts: 3.13 us -> 0.82 us
    pallas_call x1, Pallas kernels: 82.4 us -> 68.3 us  [local(): pl.pallas_call(functools.partial(mega, n), out_shape=(jax.ShapeDtypeStruc...]
    convert_element_type x0 -> x2, other arithmetic: none -> 4.9 us  [the longest x1 4.9 us: local(): return jnp.where(frame < norm[2], jax.nn.silu(normed), 0.0).astype(BF16)]
    unnamed x1 -> x2, local copies, waits for them, and re-layouts: 3.13 us -> 0.01 us
where the time goes in v2:
time: 74.2 us; the launch traced here: 74 us
  Pallas kernels  68.3 us (92%)
  other arithmetic  4.9 us (7%)
  local copies, waits for them, and re-layouts  0.82 us (1%)
    pallas_call x1, Pallas kernels, local(): pl.pallas_call(functools.partial(mega, n), out_shape=(jax.ShapeDtypeStruc...  68.3 us
    convert_element_type x1, other arithmetic, local(): return jnp.where(frame < norm[2], jax.nn.silu(normed), 0.0).astype(BF16)  4.9 us

profile of v2, /device:TPU:0, one launch (start us, length us, event | category | flops | bytes accessed | tf_op | source)
XLA Modules:
  0.0 74.0 jit_solution(17569697530125195678)
XLA Ops:
  0.0 0.0 copy-start
  0.0 68.3 %shard_map.91 = (f32[16,2,128,256]{3,2,1,0:T(8,128)}, f32[8,256]{1,0:T(8,128)}) custom-call(bf16[1024,512]{1,0:T(8,128)(2,1)} %tokens_hbm.1, bf16[512,1536]{1,0:T(8,128)(2,1)} %qkv_hbm.1, bf16[512,1024]{1,0:T(8,128)(2,1)} %out_hbm.1, bf16[3,768,256]{2,1,0:T(8,128)(2,1)} %bitcast.6, f32[1,256]{1,0:T(1,128)} %bitcast.11, s32[16]{0:T(128)} %group_ref.1, ...), custom_call_target="tpu_custom_call" | custom-call | tf_op jit(solution)/shard_map/pallas_call | solution.py:553
  68.3 0.8 %fusion = (f32[1,256]{1,0:T(1,128)S(1)}, f32[1,256]{1,0:T(1,128)S(1)}, f32[1,256]{1,0:T(1,128)S(1)}) fusion(f32[8,256]{1,0:T(8,128)} %get-tuple-element.7), kind=kLoop, calls=%fused_computation.2 | loop fusion | bytes 6144 | tf_op jit(solution)/shard_map/slice | solution.py:611
  69.1 0.0 copy-done
  69.1 4.9 %select_convert_fusion = bf16[16,2,128,256]{3,2,1,0:T(8,128)(2,1)} fusion(f32[16,2,128,256]{3,2,1,0:T(8,128)} %get-tuple-element.8, f32[256]{0:T(256)S(1)} %copy-done, f32[256]{0:T(256)S(1)} %bitcast.9, f32[256]{0:T(256)S(1)} %bitcast.10, f32[256]{0:T(256)S(1)} %bitcast.8, f32[16]{0:T(128)S(1)} %iota_convert_fusion), kind=kLoop, calls=%fused_computation | loop fusion | flops 10485760 | bytes 6295616 | tf_op jit(solution)/shard_map/convert_element_type | solution.py:611
  (1 shorter events, 0.0 us)
Async XLA Ops:
  0.0 69.1 %copy-start = (f32[256]{0:T(256)S(1)}, f32[256]{0:T(256)}, u32[]{:S(2)}) copy-start(f32[256]{0:T(256)} %param.14) | copy-start | bytes 3076

commit v3 on v2

--- a/solution.py
+++ b/solution.py
@@ -172,6 +172,30 @@
     far = half - near
 
     loads[0].wait()
+
+    @pl.loop(0, chunks)
+    def _(to):
+        place = lax.broadcasted_iota(jnp.int32, (CHUNK, count), 0) + to * CHUNK
+        pick = jnp.where(order_ref[...] == place, 1.0, 0.0).astype(BF16)
+        moved = jnp.dot(pick, tokens_ref[...], preferred_element_type=F32)
+        sent_tokens[pl.ds(to * frames_per, frames_per)] = moved.reshape(
+            frames_per, row_tokens, width
+        ).astype(BF16)
+
+    pl.semaphore_wait(barrier, n - 1)
+
+    def send_tokens(first, start, stop):
+        @pl.loop(start, stop)
+        def _(k):
+            t = first * frames_per + lax.rem(me + k, n // 2)
+
+            @pl.when(t != me)
+            def _():
+                tok_copy(t).start()
+
+    send_tokens(far, 0, n // 4)
+    tile_tokens[me] = sent_tokens[me]
+
     loads[1].wait()
     state_acc[...] = jnp.zeros_like(state_acc)
     sum_acc[...] = jnp.zeros_like(sum_acc)
@@ -214,8 +238,6 @@
     sum_at = pieces * head_dim
     sent_state[sum_at : sum_at + 16, :] = packed.astype(BF16)
 
-    pl.semaphore_wait(barrier, n - 1)
-
     @pl.loop(1, n // 2)
     def _(k):
         state_copy(k).start()
@@ -223,26 +245,8 @@
     own_pass.start()
     all_state[me] = sent_state[...]
 
-    @pl.loop(0, chunks)
-    def _(to):
-        place = lax.broadcasted_iota(jnp.int32, (CHUNK, count), 0) + to * CHUNK
-        pick = jnp.where(order_ref[...] == place, 1.0, 0.0).astype(BF16)
-        moved = jnp.dot(pick, tokens_ref[...], preferred_element_type=F32)
-        sent_tokens[pl.ds(to * frames_per, frames_per)] = moved.reshape(
-            frames_per, row_tokens, width
-        ).astype(BF16)
-
-    for first in (far, near):
-
-        @pl.loop(0, n // 2)
-        def _(k):
-            t = first * frames_per + lax.rem(me + k, n // 2)
-
-            @pl.when(t != me)
-            def _():
-                tok_copy(t).start()
-
-    tile_tokens[me] = sent_tokens[me]
+    send_tokens(near, 0, n // 2)
+    send_tokens(far, n // 4, n // 2)
 
     @pl.loop(1, n // 2)
     def _(k):
@@ -371,6 +375,8 @@
         def _():
             up_copy(c).start()
 
+    def convolve(c):
+        rows = pl.ds(pl.multiple_of(c * CHUNK, CHUNK), CHUNK)
         for r in range(2):
             for b in range(2):
                 lanes = slice(b * channels, b * channels + reach)
@@ -381,10 +387,15 @@
     @pl.loop(0, half)
     def _(k):
         advance(near + k)
+        convolve(near + k)
 
     @pl.loop(0, half)
     def _(k):
         advance(far + k)
+
+    @pl.loop(0, half)
+    def _(k):
+        convolve(far + k)
 
     @pl.when(me == 0)
     def _():

time: 74.2 us -> 75.1 us (1.012)
  Pallas kernels: 68.3 us -> 69.2 us
    pallas_call x1, Pallas kernels: 68.3 us -> 69.2 us  [local(): pl.pallas_call(functools.partial(mega, n), out_shape=(jax.ShapeDtypeStruc...]
where the time goes in v3:
time: 75.1 us; the launch traced here: 74.9 us
  Pallas kernels  69.2 us (92%)
  other arithmetic  4.9 us (7%)
  local copies, waits for them, and re-layouts  0.82 us (1%)
    pallas_call x1, Pallas kernels, local(): pl.pallas_call(functools.partial(mega, n), out_shape=(jax.ShapeDtypeStruc...  69.2 us
    convert_element_type x1, other arithmetic, local(): return jnp.where(frame < norm[2], jax.nn.silu(normed), 0.0).astype(BF16)  4.9 us

profile of v3, /device:TPU:0, one launch (start us, length us, event | category | flops | bytes accessed | tf_op | source)
XLA Modules:
  0.0 74.9 jit_solution(7932192878229867721)
XLA Ops:
  0.0 0.0 copy-start
  0.0 69.2 %shard_map.91 = (f32[16,2,128,256]{3,2,1,0:T(8,128)}, f32[8,256]{1,0:T(8,128)}) custom-call(bf16[1024,512]{1,0:T(8,128)(2,1)} %tokens_hbm.1, bf16[512,1536]{1,0:T(8,128)(2,1)} %qkv_hbm.1, bf16[512,1024]{1,0:T(8,128)(2,1)} %out_hbm.1, bf16[3,768,256]{2,1,0:T(8,128)(2,1)} %bitcast.6, f32[1,256]{1,0:T(1,128)} %bitcast.11, s32[16]{0:T(128)} %group_ref.1, ...), custom_call_target="tpu_custom_call" | custom-call | tf_op jit(solution)/shard_map/pallas_call | solution.py:564
  69.2 0.8 %fusion = (f32[1,256]{1,0:T(1,128)S(1)}, f32[1,256]{1,0:T(1,128)S(1)}, f32[1,256]{1,0:T(1,128)S(1)}) fusion(f32[8,256]{1,0:T(8,128)} %get-tuple-element.7), kind=kLoop, calls=%fused_computation.2 | loop fusion | bytes 6144 | tf_op jit(solution)/shard_map/slice | solution.py:622
  70.0 0.0 copy-done
  70.0 4.9 %select_convert_fusion = bf16[16,2,128,256]{3,2,1,0:T(8,128)(2,1)} fusion(f32[16,2,128,256]{3,2,1,0:T(8,128)} %get-tuple-element.8, f32[256]{0:T(256)S(1)} %copy-done, f32[256]{0:T(256)S(1)} %bitcast.9, f32[256]{0:T(256)S(1)} %bitcast.10, f32[256]{0:T(256)S(1)} %bitcast.8, f32[16]{0:T(128)S(1)} %iota_convert_fusion), kind=kLoop, calls=%fused_computation | loop fusion | flops 10485760 | bytes 6295616 | tf_op jit(solution)/shard_map/convert_element_type | solution.py:622
  (1 shorter events, 0.0 us)
Async XLA Ops:
  0.0 70.0 %copy-start = (f32[256]{0:T(256)S(1)}, f32[256]{0:T(256)}, u32[]{:S(2)}) copy-start(f32[256]{0:T(256)} %param.14) | copy-start | bytes 3076

commit v4 on v2

--- a/solution.py
+++ b/solution.py
@@ -232,7 +232,7 @@
             frames_per, row_tokens, width
         ).astype(BF16)
 
-    for first in (far, near):
+    for first in (near, far):
 
         @pl.loop(0, n // 2)
         def _(k):

time: 74.2 us -> 70.8 us (0.954)
  Pallas kernels: 68.3 us -> 64.8 us
    pallas_call x1, Pallas kernels: 68.3 us -> 64.8 us  [local(): pl.pallas_call(functools.partial(mega, n), out_shape=(jax.ShapeDtypeStruc...]
where the time goes in v4:
time: 70.8 us; the launch traced here: 70.6 us
  Pallas kernels  64.8 us (92%)
  other arithmetic  4.9 us (7%)
  local copies, waits for them, and re-layouts  0.82 us (1%)
    pallas_call x1, Pallas kernels, local(): pl.pallas_call(functools.partial(mega, n), out_shape=(jax.ShapeDtypeStruc...  64.8 us
    convert_element_type x1, other arithmetic, local(): return jnp.where(frame < norm[2], jax.nn.silu(normed), 0.0).astype(BF16)  4.9 us

profile of v4, /device:TPU:0, one launch (start us, length us, event | category | flops | bytes accessed | tf_op | source)
XLA Modules:
  0.0 70.6 jit_solution(5215081791993592138)
XLA Ops:
  0.0 0.0 copy-start
  0.0 64.8 %shard_map.91 = (f32[16,2,128,256]{3,2,1,0:T(8,128)}, f32[8,256]{1,0:T(8,128)}) custom-call(bf16[1024,512]{1,0:T(8,128)(2,1)} %tokens_hbm.1, bf16[512,1536]{1,0:T(8,128)(2,1)} %qkv_hbm.1, bf16[512,1024]{1,0:T(8,128)(2,1)} %out_hbm.1, bf16[3,768,256]{2,1,0:T(8,128)(2,1)} %bitcast.6, f32[1,256]{1,0:T(1,128)} %bitcast.11, s32[16]{0:T(128)} %group_ref.1, ...), custom_call_target="tpu_custom_call" | custom-call | tf_op jit(solution)/shard_map/pallas_call | solution.py:553
  64.8 0.8 %fusion = (f32[1,256]{1,0:T(1,128)S(1)}, f32[1,256]{1,0:T(1,128)S(1)}, f32[1,256]{1,0:T(1,128)S(1)}) fusion(f32[8,256]{1,0:T(8,128)} %get-tuple-element.7), kind=kLoop, calls=%fused_computation.2 | loop fusion | bytes 6144 | tf_op jit(solution)/shard_map/slice | solution.py:611
  65.7 0.0 copy-done
  65.7 4.9 %select_convert_fusion = bf16[16,2,128,256]{3,2,1,0:T(8,128)(2,1)} fusion(f32[16,2,128,256]{3,2,1,0:T(8,128)} %get-tuple-element.8, f32[256]{0:T(256)S(1)} %copy-done, f32[256]{0:T(256)S(1)} %bitcast.9, f32[256]{0:T(256)S(1)} %bitcast.10, f32[256]{0:T(256)S(1)} %bitcast.8, f32[16]{0:T(128)S(1)} %iota_convert_fusion), kind=kLoop, calls=%fused_computation | loop fusion | flops 10485760 | bytes 6295616 | tf_op jit(solution)/shard_map/convert_element_type | solution.py:611
  (1 shorter events, 0.0 us)
Async XLA Ops:
  0.0 65.7 %copy-start = (f32[256]{0:T(256)S(1)}, f32[256]{0:T(256)}, u32[]{:S(2)}) copy-start(f32[256]{0:T(256)} %param.14) | copy-start | bytes 3076
